TPU v7x, 32 devices: a whole 2x2x4 slice. The times are simulated.
32 devices in a mesh: dp: 4 (over y, x), ctx: 8 (over z, core).
Axes of the slice: x: 2, y: 2, z: 4, core: 2. Of those that a mesh axis runs over, the one named last changes fastest.
Arguments:
- tokens: bfloat16 [8, 2048, 1024], P('dp', 'ctx'), may hold values from -6 to 6
- positions: int32 [8, 2048], P('dp'), may hold values from 0 to 2047, as said below
- w_query: bfloat16 [1024, 2048], P(('dp', 'ctx')), may hold values from -0.1875 to 0.1875
- w_key: bfloat16 [1024, 1024], P(('dp', 'ctx')), may hold values from -0.1875 to 0.1875
- w_value: bfloat16 [1024, 1024], P(('dp', 'ctx')), may hold values from -0.1875 to 0.1875
- w_out: bfloat16 [2048, 1024], P(('dp', 'ctx')), may hold values from -1 to 1
- w_gate: bfloat16 [1024, 3072], P(('dp', 'ctx')), may hold values from -0.1875 to 0.1875
- w_up: bfloat16 [1024, 3072], P(('dp', 'ctx')), may hold values from -0.1875 to 0.1875
- w_down: bfloat16 [3072, 1024], P(('dp', 'ctx')), may hold values from -0.109375 to 0.109375
- attn_gain: bfloat16 [1024], P(('dp', 'ctx')), may hold values from 0.5 to 1.5
- mlp_gain: bfloat16 [1024], P(('dp', 'ctx')), may hold values from 0.5 to 1.5
- q_gain: bfloat16 [128], P(('dp', 'ctx')), may hold values from 0.5 to 1.5
- k_gain: bfloat16 [128], P(('dp', 'ctx')), may hold values from 0.5 to 1.5
- grad_out: bfloat16 [8, 2048, 1024], P('dp', 'ctx'), may hold values from -6 to 6
Outputs:
- output: bfloat16 [8, 2048, 1024], P('dp', 'ctx')
- input_grad: bfloat16 [8, 2048, 1024], P('dp', 'ctx')
- grad_w_query: float32 [1024, 2048], P(('dp', 'ctx'))
- grad_w_key: float32 [1024, 1024], P(('dp', 'ctx'))
- grad_w_value: float32 [1024, 1024], P(('dp', 'ctx'))
- grad_w_out: float32 [2048, 1024], P(('dp', 'ctx'))
- grad_w_gate: float32 [1024, 3072], P(('dp', 'ctx'))
- grad_w_up: float32 [1024, 3072], P(('dp', 'ctx'))
- grad_w_down: float32 [3072, 1024], P(('dp', 'ctx'))
- grad_attn_gain: float32 [1024], P(('dp', 'ctx'))
- grad_mlp_gain: float32 [1024], P(('dp', 'ctx'))
- grad_q_gain: float32 [128], P(('dp', 'ctx'))
- grad_k_gain: float32 [128], P(('dp', 'ctx'))
Inputs may be any that keep to these rules, and one draw needn't show every extreme that they name: Each row is a permutation of 0 to 2047 made of 16 blocks of 128 consecutive positions in rising order; slots j * 2 * 128 to (j + 1) * 2 * 128 - 1 hold block c followed by block 15 - c, c drawn per row and per j.
All inputs are finite; a program needn't handle non-finite values.
Results may differ from a plain program's by a relative error of at most 0.023.
Values may be sent and summed in bfloat16 or wider, within the bound.
A program may use at most 384 MiB of HBM per device.

v0:
```python
import jax
import jax.numpy as jnp
from jax import lax
from jax.sharding import PartitionSpec as P

H = 16
KV = 8
HD = 128
SEQ = 2048
MICRO = 2
SEQ_MB = 1
EPSILON = 1e-06
THETA = 1000000.0
NEGATIVE = -1e30


def normed(values, weights):
    return values * lax.rsqrt(jnp.mean(values * values, axis=-1, keepdims=True) + EPSILON) * weights


def angle_tables(position_ids):
    half_width = HD // 2
    inverse = THETA ** (-(jnp.arange(half_width).astype(jnp.float32) * 2.0 / HD))
    angles = position_ids.astype(jnp.float32)[:, None] * inverse[None, :]
    angles = jnp.concatenate([angles, angles], axis=-1)
    return (jnp.cos(angles), jnp.sin(angles))


def rotated(values, cosine, sine_table):
    half_width = values.shape[-1] // 2
    turned = jnp.concatenate([-values[..., half_width:], values[..., :half_width]], axis=-1)
    return values * cosine + turned * sine_table


def prepared(raw_rows, gain_vector, cosine, sine_table):
    row_count = raw_rows.shape[0]
    heads = raw_rows.reshape(row_count, -1, HD)
    return rotated(normed(heads, gain_vector), cosine[:, None], sine_table[:, None]).reshape(
        row_count, -1
    )


def scored(query_heads, keys_all, causal):
    result = jnp.einsum(
        "bqkgd,bskd->bkgqs", query_heads, keys_all, preferred_element_type=jnp.float32
    ) * HD ** (-0.5)
    return jnp.where(causal[:, None, None], result, NEGATIVE)


def accumulate(totals, new_items):
    if totals is None:
        return new_items
    return tuple((total_item + new_item for total_item, new_item in zip(totals, new_items)))


def shards(
    tokens,
    positions,
    w_query,
    w_key,
    w_value,
    w_out,
    w_gate,
    w_up,
    w_down,
    attn_gain,
    mlp_gain,
    q_gain,
    k_gain,
    grad_out,
):
    shard_slots = tokens.shape[1]
    model_width = tokens.shape[2]
    ctx_index = lax.axis_index("ctx")
    groups = H // KV
    row_count = SEQ_MB * shard_slots
    attn_totals = None
    mlp_totals = None
    outputs = []
    input_grads = []
    for micro_step in range(MICRO):
        first_seq = micro_step * SEQ_MB
        block_tokens = tokens[first_seq : first_seq + SEQ_MB]
        block_cotangent = grad_out[first_seq : first_seq + SEQ_MB]
        whole_pos = positions[first_seq : first_seq + SEQ_MB]
        own_pos = lax.dynamic_slice_in_dim(whole_pos, ctx_index * shard_slots, shard_slots, 1)
        causal = whole_pos[:, None, :] <= own_pos[:, :, None]
        cosine, sine_table = angle_tables(own_pos.reshape(row_count))
        residual_in = block_tokens.reshape(row_count, model_width).astype(jnp.float32)
        full_query, full_key, full_value, full_out, full_attn_gain, full_q_gain, full_k_gain = (
            lax.all_gather(w_query, ("dp", "ctx"), axis=0, tiled=True),
            lax.all_gather(w_key, ("dp", "ctx"), axis=0, tiled=True),
            lax.all_gather(w_value, ("dp", "ctx"), axis=0, tiled=True),
            lax.all_gather(w_out, ("dp", "ctx"), axis=0, tiled=True),
            lax.all_gather(attn_gain, ("dp", "ctx"), axis=0, tiled=True),
            lax.all_gather(q_gain, ("dp", "ctx"), axis=0, tiled=True),
            lax.all_gather(k_gain, ("dp", "ctx"), axis=0, tiled=True),
        )
        gain_attn = full_attn_gain.astype(jnp.float32)
        query_gain = full_q_gain.astype(jnp.float32)
        key_gain = full_k_gain.astype(jnp.float32)
        hidden = normed(residual_in, gain_attn).astype(jnp.bfloat16)
        query_raw = jnp.dot(hidden, full_query, preferred_element_type=jnp.float32)
        key_raw = jnp.dot(hidden, full_key, preferred_element_type=jnp.float32)
        value_raw = jnp.dot(hidden, full_value, preferred_element_type=jnp.float32)
        queries = prepared(query_raw, query_gain, cosine, sine_table).astype(jnp.bfloat16)
        keys_own = prepared(key_raw, key_gain, cosine, sine_table).astype(jnp.bfloat16)
        values_own = value_raw.astype(jnp.bfloat16)
        keys_all, values_all = (
            lax.all_gather(
                keys_own.reshape(SEQ_MB, shard_slots, KV * HD), "ctx", axis=1, tiled=True
            ),
            lax.all_gather(
                values_own.reshape(SEQ_MB, shard_slots, KV * HD), "ctx", axis=1, tiled=True
            ),
        )
        keys_all = keys_all.reshape(SEQ_MB, SEQ, KV, HD)
        values_all = values_all.reshape(SEQ_MB, SEQ, KV, HD)
        query_heads = queries.reshape(SEQ_MB, shard_slots, KV, groups, HD)
        scores = scored(query_heads, keys_all, causal)
        top_score = jnp.max(scores, axis=-1, keepdims=True)
        log_total = top_score + jnp.log(
            jnp.sum(jnp.exp(scores - top_score), axis=-1, keepdims=True)
        )
        prob_low = jnp.exp(scores - log_total).astype(jnp.bfloat16)
        mixed_heads = jnp.einsum(
            "bkgqs,bskd->bqkgd", prob_low, values_all, preferred_element_type=jnp.float32
        )
        mixed_rows = mixed_heads.reshape(row_count, H * HD).astype(jnp.bfloat16)
        middle = residual_in + jnp.dot(mixed_rows, full_out, preferred_element_type=jnp.float32)
        full_gate, full_up, full_down, full_mlp_gain = (
            lax.all_gather(w_gate, ("dp", "ctx"), axis=0, tiled=True),
            lax.all_gather(w_up, ("dp", "ctx"), axis=0, tiled=True),
            lax.all_gather(w_down, ("dp", "ctx"), axis=0, tiled=True),
            lax.all_gather(mlp_gain, ("dp", "ctx"), axis=0, tiled=True),
        )
        gain_mlp = full_mlp_gain.astype(jnp.float32)
        second = normed(middle, gain_mlp).astype(jnp.bfloat16)
        gate_proj = jnp.dot(second, full_gate, preferred_element_type=jnp.float32)
        up_proj = jnp.dot(second, full_up, preferred_element_type=jnp.float32)
        sigmoid_gate = jax.nn.sigmoid(gate_proj)
        silu_gate = gate_proj * sigmoid_gate
        activated = (silu_gate * up_proj).astype(jnp.bfloat16)
        result_rows = middle + jnp.dot(activated, full_down, preferred_element_type=jnp.float32)
        outputs.append(result_rows.astype(jnp.bfloat16).reshape(SEQ_MB, shard_slots, model_width))
        cotangent = block_cotangent.reshape(row_count, model_width).astype(jnp.float32)
        full_gate, full_up, full_down = (full_gate, full_up, full_down)
        down_grad_in = block_cotangent.reshape(row_count, model_width)
        grad_down_w = jnp.einsum(
            "rf,rd->fd", activated, down_grad_in, preferred_element_type=jnp.float32
        )
        grad_act = jnp.einsum(
            "rd,fd->rf", down_grad_in, full_down, preferred_element_type=jnp.float32
        )
        grad_gate = (
            grad_act * up_proj * sigmoid_gate * (1.0 + gate_proj * (1.0 - sigmoid_gate))
        ).astype(jnp.bfloat16)
        grad_up_rows = (grad_act * silu_gate).astype(jnp.bfloat16)
        grad_gate_w = jnp.einsum("rd,rf->df", second, grad_gate, preferred_element_type=jnp.float32)
        grad_up_w = jnp.einsum(
            "rd,rf->df", second, grad_up_rows, preferred_element_type=jnp.float32
        )
        grad_second = jnp.einsum(
            "rf,df->rd", grad_gate, full_gate, preferred_element_type=jnp.float32
        ) + jnp.einsum("rf,df->rd", grad_up_rows, full_up, preferred_element_type=jnp.float32)
        _, mlp_pull = jax.vjp(normed, middle, gain_mlp)
        grad_middle_part, grad_mlp_gain = mlp_pull(grad_second)
        grad_middle = cotangent + grad_middle_part
        mlp_totals = accumulate(mlp_totals, (grad_gate_w, grad_up_w, grad_down_w, grad_mlp_gain))
        full_query, full_key, full_value, full_out = (full_query, full_key, full_value, full_out)
        attn_grad_in = grad_middle.astype(jnp.bfloat16)
        grad_out_w = jnp.einsum(
            "rh,rd->hd", mixed_rows, attn_grad_in, preferred_element_type=jnp.float32
        )
        grad_mixed = jnp.einsum(
            "rd,hd->rh", attn_grad_in, full_out, preferred_element_type=jnp.float32
        ).astype(jnp.bfloat16)
        grad_heads = grad_mixed.reshape(SEQ_MB, shard_slots, KV, groups, HD)
        scores = scored(query_heads, keys_all, causal)
        weights_full = jnp.exp(scores - log_total)
        grad_probs = jnp.einsum(
            "bqkgd,bskd->bkgqs", grad_heads, values_all, preferred_element_type=jnp.float32
        )
        row_sum = jnp.sum(weights_full * grad_probs, axis=-1, keepdims=True)
        grad_scores = (weights_full * (grad_probs - row_sum)).astype(jnp.bfloat16)
        grad_query = jnp.einsum(
            "bkgqs,bskd->bqkgd", grad_scores, keys_all, preferred_element_type=jnp.float32
        ) * HD ** (-0.5)
        weights_low = weights_full.astype(jnp.bfloat16)
        key_part = jnp.einsum(
            "bkgqs,bqkgd->bskd", grad_scores, query_heads, preferred_element_type=jnp.float32
        ) * HD ** (-0.5)
        value_part = jnp.einsum(
            "bkgqs,bqkgd->bskd", weights_low, grad_heads, preferred_element_type=jnp.float32
        )
        key_sum, value_sum = (
            lax.psum_scatter(
                key_part.reshape(SEQ_MB, SEQ, KV * HD).astype(jnp.bfloat16),
                "ctx",
                scatter_dimension=1,
                tiled=True,
            ).astype(jnp.float32),
            lax.psum_scatter(
                value_part.reshape(SEQ_MB, SEQ, KV * HD).astype(jnp.bfloat16),
                "ctx",
                scatter_dimension=1,
                tiled=True,
            ).astype(jnp.float32),
        )
        _, key_pull = jax.vjp(
            lambda raw_rows, gain_vector: prepared(raw_rows, gain_vector, cosine, sine_table),
            key_raw,
            key_gain,
        )
        grad_key_raw, grad_key_gain = key_pull(key_sum.reshape(row_count, KV * HD))
        _, query_pull = jax.vjp(
            lambda raw_rows, gain_vector: prepared(raw_rows, gain_vector, cosine, sine_table),
            query_raw,
            query_gain,
        )
        grad_query_raw, grad_query_gain = query_pull(grad_query.reshape(row_count, H * HD))
        grad_query_low = grad_query_raw.astype(jnp.bfloat16)
        grad_key_low = grad_key_raw.astype(jnp.bfloat16)
        grad_value_low = value_sum.reshape(row_count, KV * HD).astype(jnp.bfloat16)
        grad_query_w = jnp.einsum(
            "rd,rh->dh", hidden, grad_query_low, preferred_element_type=jnp.float32
        )
        grad_key_w = jnp.einsum(
            "rd,rh->dh", hidden, grad_key_low, preferred_element_type=jnp.float32
        )
        grad_value_w = jnp.einsum(
            "rd,rh->dh", hidden, grad_value_low, preferred_element_type=jnp.float32
        )
        grad_hidden = jnp.einsum(
            "rh,dh->rd", grad_query_low, full_query, preferred_element_type=jnp.float32
        )
        grad_hidden = grad_hidden + jnp.einsum(
            "rh,dh->rd", grad_key_low, full_key, preferred_element_type=jnp.float32
        )
        grad_hidden = grad_hidden + jnp.einsum(
            "rh,dh->rd", grad_value_low, full_value, preferred_element_type=jnp.float32
        )
        _, attn_pull = jax.vjp(normed, residual_in, gain_attn)
        grad_input_part, grad_attn_gain = attn_pull(grad_hidden)
        input_grads.append(
            (grad_middle + grad_input_part)
            .astype(jnp.bfloat16)
            .reshape(SEQ_MB, shard_slots, model_width)
        )
        attn_totals = accumulate(
            attn_totals,
            (
                grad_query_w,
                grad_key_w,
                grad_value_w,
                grad_out_w,
                grad_attn_gain,
                grad_query_gain,
                grad_key_gain,
            ),
        )
    mlp_sums = lax.psum_scatter(mlp_totals, ("dp", "ctx"), scatter_dimension=0, tiled=True)
    attn_sums = lax.psum_scatter(attn_totals, ("dp", "ctx"), scatter_dimension=0, tiled=True)
    output_all = jnp.concatenate(outputs, axis=0)
    input_all = jnp.concatenate(input_grads, axis=0)
    return (
        output_all,
        input_all,
        attn_sums[0],
        attn_sums[1],
        attn_sums[2],
        attn_sums[3],
        mlp_sums[0],
        mlp_sums[1],
        mlp_sums[2],
        attn_sums[4],
        mlp_sums[3],
        attn_sums[5],
        attn_sums[6],
    )


def solution(mesh):
    in_specs = (
        P("dp", "ctx", None),
        P("dp", None),
        P(("dp", "ctx"), None),
        P(("dp", "ctx"), None),
        P(("dp", "ctx"), None),
        P(("dp", "ctx"), None),
        P(("dp", "ctx"), None),
        P(("dp", "ctx"), None),
        P(("dp", "ctx"), None),
        P(("dp", "ctx")),
        P(("dp", "ctx")),
        P(("dp", "ctx")),
        P(("dp", "ctx")),
        P("dp", "ctx", None),
    )
    out_specs = (
        P("dp", "ctx", None),
        P("dp", "ctx", None),
        P(("dp", "ctx"), None),
        P(("dp", "ctx"), None),
        P(("dp", "ctx"), None),
        P(("dp", "ctx"), None),
        P(("dp", "ctx"), None),
        P(("dp", "ctx"), None),
        P(("dp", "ctx"), None),
        P(("dp", "ctx")),
        P(("dp", "ctx")),
        P(("dp", "ctx")),
        P(("dp", "ctx")),
    )
    return jax.shard_map(shards, mesh=mesh, in_specs=in_specs, out_specs=out_specs, check_vma=False)
```

profile of v0, /device:TPU:0, one launch (start us, length us, event | category | flops | bytes accessed | tf_op | source)
XLA Modules:
  0.0 2012.8 jit_solution(11946247957743827104)
XLA Ops:
  12.8 42.3 %all-reduce.17 = (bf16[1024]{0:T(1024)(128)(2,1)S(1)}, bf16[128]{0:T(256)(128)(2,1)S(1)}, bf16[128]{0:T(256)(128)(2,1)S(1)}, bf16[1024]{0:T(1024)(128)(2,1)S(1)}) all-reduce(bf16[1024]{0:T(1024)(128)(2,1)S(1)} %dynamic-update-slice, bf16[128]{0:T(256)(128)(2,1)S(1)} %dynamic-update-slice.1, ...), channel_id=1, replica_groups=mesh['dp'=4,'ctx'=8] {'dp','ctx'}, use_global_device_ids=true, to_apply=%add.8 | all-reduce | flops 2304 | bytes 9216
  58.7 11.5 all-gather.16.cloned.1.call-done
  79.3 49.3 %all-gather.14.cloned.1.call-done = bf16[1024,1024]{1,0:T(8,128)(2,1)} async-done(((bf16[32,1024]{1,0:T(8,128)(2,1)}), bf16[1024,1024]{1,0:T(8,128)(2,1)}) %all-gather.14.cloned.1.call-update) | async-done | bytes 2097168 | tf_op jit(solution)/shard_map/all_gather | solution.py:93
  140.6 52.0 %all-gather.20.cloned.1.call-done = bf16[1024,2048]{1,0:T(8,128)(2,1)} async-done(((bf16[32,2048]{1,0:T(8,128)(2,1)}), bf16[1024,2048]{1,0:T(8,128)(2,1)}) %all-gather.20.cloned.1.call-update) | async-done | bytes 4194320 | tf_op jit(solution)/shard_map/all_gather | solution.py:91
  192.6 6.4 copy.72
  208.7 31.7 %all-gather.30.cloned.1.call-done = bf16[1,2048,1024]{1,2,0:T(8,128)(2,1)} async-done(((bf16[1,256,1024]{1,2,0:T(8,128)(2,1)}), bf16[1,2048,1024]{1,2,0:T(8,128)(2,1)}) %all-gather.30.cloned.1.call-update) | async-done | bytes 4194320 | tf_op jit(solution)/shard_map/all_gather | solution.py:110
  240.4 16.0 fusion.9
  256.4 14.5 exponential_reduce_fusion
  270.9 16.9 all-gather.34.cloned.1.call-done
  287.9 5.2 copy.130
  293.1 42.1 %all-gather.32.cloned.1.call-done = bf16[2048,1024]{1,0:T(8,128)(2,1)} async-done(((bf16[256,1024]{1,0:T(8,128)(2,1)}), bf16[2048,1024]{1,0:T(8,128)(2,1)}) %all-gather.32.cloned.1.call-update) | async-done | bytes 4194320 | tf_op jit(solution)/shard_map/all_gather | solution.py:113
  335.2 5.3 copy.129
  340.5 17.6 fusion.39
  358.1 41.0 %all-gather.22.cloned.1.call-done = bf16[2048,1024]{1,0:T(8,128)(2,1)} async-done(((bf16[64,1024]{1,0:T(8,128)(2,1)}), bf16[2048,1024]{1,0:T(8,128)(2,1)}) %all-gather.22.cloned.1.call-update) | async-done | bytes 4194320 | tf_op jit(solution)/shard_map/all_gather | solution.py:94
  403.9 43.2 %all-gather.18.cloned.1.call-done = bf16[1,2048,1024]{1,2,0:T(8,128)(2,1)} async-done(((bf16[1,256,1024]{1,2,0:T(8,128)(2,1)}), bf16[1,2048,1024]{1,2,0:T(8,128)(2,1)}) %all-gather.18.cloned.1.call-update) | async-done | bytes 4194320 | tf_op jit(solution)/shard_map/all_gather | solution.py:110
  447.1 16.3 fusion.8
  463.4 14.5 exponential_reduce_fusion.1
  477.9 17.2 fusion.36
  499.2 18.6 all-gather.26.cloned.1.call-done
  517.8 6.3 fusion.177
  524.1 64.5 %all-gather.24.cloned.1.call-done = bf16[1024,3072]{1,0:T(8,128)(2,1)} async-done(((bf16[32,3072]{1,0:T(8,128)(2,1)}), bf16[1024,3072]{1,0:T(8,128)(2,1)}) %all-gather.24.cloned.1.call-update) | async-done | bytes 6291472 | tf_op jit(solution)/shard_map/all_gather | solution.py:132
  588.6 6.3 fusion.176
  594.9 64.7 %all-gather.28.cloned.1.call-done = bf16[3072,1024]{1,0:T(8,128)(2,1)} async-done(((bf16[96,1024]{1,0:T(8,128)(2,1)}), bf16[3072,1024]{1,0:T(8,128)(2,1)}) %all-gather.28.cloned.1.call-update) | async-done | bytes 6291472 | tf_op jit(solution)/shard_map/all_gather | solution.py:134
  659.6 9.0 multiply_convert_fusion.2
  670.6 6.5 multiply_reduce_fusion.9
  684.4 9.6 multiply_convert_fusion
  694.0 5.7 fusion.182
  709.2 16.8 bitcast_convert_fusion.1
  732.0 16.6 bitcast_convert_fusion
  748.7 25.8 %fusion = (f32[8,2,256]{2,1,0:T(2,128)S(1)}, f32[8,2048,256,2]{2,1,3,0:T(8,128)}) fusion(f32[8,2048,256,2]{2,1,3,0:T(8,128)} %get-tuple-element.100, f32[8,2,256]{2,1,0:T(2,128)S(1)} %bitcast.472, pred[256,2048]{0,1:T(8,128)(4,1)S(1)} %broadcast_compare_fusion, bf16[256,8,2,128]{0,3,2,1:T(8,128)(2,1)S(1)} %bitcast.444, bf16[2048,8,128,1]{2,1,0,3:T(8,128)(2,1)} %bitcast.418), kind=kOutput, calls=%fused_computation.4 | convolution fusion | flops 2189422592 | bytes 72908800 | tf_op jit(solution)/shard_map/bqkgd,bskd->bkgqs/dot_general | solution.py:181
  774.5 28.9 %fusion.13 = bf16[8,2,256,2048]{2,3,1,0:T(8,128)(2,1)} fusion(f32[8,2048,256,2]{2,1,3,0:T(8,128)} %get-tuple-element.112, f32[8,2048,256,2]{2,1,3,0:T(8,128)} %get-tuple-element.100, f32[8,2,256]{2,1,0:T(2,128)S(1)} %get-tuple-element.111, f32[8,2,256]{2,1,0:T(2,128)S(1)} %bitcast.473, pred[256,2048]{0,1:T(8,128)(4,1)S(1)} %broadcast_compare_fusion), kind=kLoop, calls=%fused_computation.23 | loop fusion | flops 50331648 | bytes 84443136 | tf_op jit(solution)/shard_map/reshape.45
  803.4 10.5 fusion.14
  815.1 25.6 %fusion.3 = (f32[8,2,256]{2,1,0:T(2,128)S(1)}, f32[8,2048,256,2]{2,1,3,0:T(8,128)}) fusion(f32[8,2048,256,2]{2,1,3,0:T(8,128)} %get-tuple-element.102, f32[8,2,256]{2,1,0:T(2,128)S(1)} %bitcast.468, pred[256,2048]{0,1:T(8,128)(4,1)S(1)} %broadcast_compare_fusion.1, bf16[256,8,2,128]{0,3,2,1:T(8,128)(2,1)S(1)} %bitcast.442, ...), kind=kOutput, calls=%fused_computation.9 | convolution fusion | flops 2189422592 | bytes 72908800 | tf_op jit(solution)/shard_map/bqkgd,bskd->bkgqs/dot_general | solution.py:181
  840.7 29.0 %fusion.12 = bf16[8,2,256,2048]{2,3,1,0:T(8,128)(2,1)} fusion(f32[8,2048,256,2]{2,1,3,0:T(8,128)} %get-tuple-element.110, f32[8,2048,256,2]{2,1,3,0:T(8,128)} %get-tuple-element.102, f32[8,2,256]{2,1,0:T(2,128)S(1)} %get-tuple-element.109, f32[8,2,256]{2,1,0:T(2,128)S(1)} %bitcast.469, pred[256,2048]{0,1:T(8,128)(4,1)S(1)} %broadcast_compare_fusion.1), kind=kLoop, calls=%fused_computation.22 | loop fusion | flops 50331648 | bytes 84443136 | tf_op jit(solution)/shard_map/reshape.28
  869.8 10.5 fusion.15
  890.9 6.5 convolution_add_fusion.1
  900.9 6.5 convolution_add_fusion.2
  911.1 6.5 convolution_add_fusion
  917.8 9.7 convolution_multiply_fusion
  970.5 5.3 fusion.59
  990.5 40.6 %all-reduce.16 = (f32[1024]{0:T(1024)S(1)}, f32[1024]{0:T(1024)S(1)}, f32[128]{0:T(128)S(1)}, f32[128]{0:T(128)S(1)}) all-reduce(f32[1024]{0:T(1024)S(1)} %add.293, f32[1024]{0:T(1024)S(1)} %add.294, f32[128]{0:T(128)S(1)} %add.295, f32[128]{0:T(128)S(1)} %add.296), channel_id=15, replica_groups=mesh['dp'=4,'ctx'=8] {'dp','ctx'}, use_global_device_ids=true, to_apply=%region_35.36.clone | all-reduce | flops 2304 | bytes 18432
  1036.7 45.9 %reduce-scatter.26.cloned.1.call-done = f32[64,1024]{1,0:T(8,128)} async-done(((f32[2048,1024]{1,0:T(8,128)}), f32[64,1024]{1,0:T(8,128)}) %reduce-scatter.26.cloned.1.call-update) | async-done | bytes 262160 | tf_op jit(solution)/shard_map/reduce_scatter | solution.py:263
  1082.6 159.5 %reduce-scatter.30.cloned.1.call-done = f32[32,3072]{1,0:T(8,128)} async-done(((f32[1024,3072]{1,0:T(8,128)}), f32[32,3072]{1,0:T(8,128)}) %reduce-scatter.30.cloned.1.call-update) | async-done | bytes 393232 | tf_op jit(solution)/shard_map/reduce_scatter | solution.py:262
  1242.2 162.3 %reduce-scatter.28.cloned.1.call-done = f32[32,3072]{1,0:T(8,128)} async-done(((f32[1024,3072]{1,0:T(8,128)}), f32[32,3072]{1,0:T(8,128)}) %reduce-scatter.28.cloned.1.call-update) | async-done | bytes 393232 | tf_op jit(solution)/shard_map/reduce_scatter | solution.py:262
  1404.4 161.4 %reduce-scatter.32.cloned.1.call-done = f32[96,1024]{1,0:T(8,128)} async-done(((f32[3072,1024]{1,0:T(8,128)}), f32[96,1024]{1,0:T(8,128)}) %reduce-scatter.32.cloned.1.call-update) | async-done | bytes 393232 | tf_op jit(solution)/shard_map/reduce_scatter | solution.py:262
  1565.8 153.8 %reduce-scatter.20.cloned.1.call-done = f32[32,2048]{1,0:T(8,128)} async-done(((f32[1024,2048]{1,0:T(8,128)}), f32[32,2048]{1,0:T(8,128)}) %reduce-scatter.20.cloned.1.call-update) | async-done | bytes 262160 | tf_op jit(solution)/shard_map/reduce_scatter | solution.py:263
  1719.6 143.8 %reduce-scatter.24.cloned.1.call-done = f32[32,1024]{1,0:T(8,128)} async-done(((f32[1024,1024]{1,0:T(8,128)}), f32[32,1024]{1,0:T(8,128)}) %reduce-scatter.24.cloned.1.call-update) | async-done | bytes 131088 | tf_op jit(solution)/shard_map/reduce_scatter | solution.py:263
  1863.4 142.3 %reduce-scatter.22.cloned.1.call-done = f32[32,1024]{1,0:T(8,128)} async-done(((f32[1024,1024]{1,0:T(8,128)}), f32[32,1024]{1,0:T(8,128)}) %reduce-scatter.22.cloned.1.call-update) | async-done | bytes 131088 | tf_op jit(solution)/shard_map/reduce_scatter | solution.py:263
  (390 shorter events, 154.4 us)
Async XLA Ops:
  7.2 67.0 %copy-start = (bf16[2,256,1024]{2,1,0:T(8,128)(2,1)S(1)}, bf16[2,256,1024]{2,1,0:T(8,128)(2,1)}, u32[]{:S(2)}) copy-start(bf16[2,256,1024]{2,1,0:T(8,128)(2,1)} %param.14) | copy-start | bytes 3145732
  7.2 63.1 %all-gather.16.cloned.1.call-start = ((), (), s32[]{:S(2)}) async-start(), calls=%async_computation.12 | async-start | bytes 2162688 | tf_op jit(solution)/shard_map/all_gather | solution.py:92
  7.9 120.7 %all-gather.14.cloned.1.call-start = ((), (), s32[]{:S(2)}) async-start(), calls=%async_computation.11 | async-start | bytes 2162688 | tf_op jit(solution)/shard_map/all_gather | solution.py:93
  8.7 183.9 %all-gather.20.cloned.1.call-start = ((), (), s32[]{:S(2)}) async-start(), calls=%async_computation.14 | async-start | bytes 4325376 | tf_op jit(solution)/shard_map/all_gather | solution.py:91
  9.4 231.0 %all-gather.30.cloned.1.call-start = ((), (), s32[]{:S(2)}) async-start(), calls=%async_computation.19 | async-start | bytes 4718592 | tf_op jit(solution)/shard_map/all_gather | solution.py:110
  55.1 22.6 %copy-start.101 = (f32[128]{0:T(128)}, f32[128]{0:T(128)S(1)}, u32[]{:S(2)}) copy-start(f32[128]{0:T(128)S(1)} %convert_element_type.362) | copy-start | bytes 1540
  55.1 148.0 %copy-start.71 = (f32[1024]{0:T(1024)}, f32[1024]{0:T(1024)S(1)}, u32[]{:S(2)}) copy-start(f32[1024]{0:T(1024)S(1)} %convert_element_type.356) | copy-start | bytes 12292
  56.6 150.7 %copy-start.29 = (f32[256,128]{0,1:T(8,128)}, f32[256,128]{0,1:T(8,128)S(1)}, u32[]{:S(2)}) copy-start(f32[256,128]{0,1:T(8,128)S(1)} %get-tuple-element.71) | copy-start | bytes 393220
  56.6 150.7 %copy-start.54 = (f32[256,128]{0,1:T(8,128)}, f32[256,128]{0,1:T(8,128)S(1)}, u32[]{:S(2)}) copy-start(f32[256,128]{0,1:T(8,128)S(1)} %get-tuple-element.72) | copy-start | bytes 393220
  58.2 18.6 copy-start.97
  58.7 144.4 %copy-start.85 = (f32[256]{0:T(256)}, f32[256]{0:T(256)S(1)}, u32[]{:S(2)}) copy-start(f32[256]{0:T(256)S(1)} %fusion.147) | copy-start | bytes 3076
  58.7 140.3 %copy-start.91 = (f32[256]{0:T(256)}, f32[256]{0:T(256)S(1)}, u32[]{:S(2)}) copy-start(f32[256]{0:T(256)S(1)} %fusion.149) | copy-start | bytes 3076
  79.2 208.7 %all-gather.34.cloned.1.call-start = ((), (), s32[]{:S(2)}) async-start(), calls=%async_computation.32 | async-start | bytes 4718592 | tf_op jit(solution)/shard_map/all_gather | solution.py:113
  131.7 203.5 %all-gather.32.cloned.1.call-start = ((), (), s32[]{:S(2)}) async-start(), calls=%async_computation.31 | async-start | bytes 4718592 | tf_op jit(solution)/shard_map/all_gather | solution.py:113
  135.0 264.1 %all-gather.22.cloned.1.call-start = ((), (), s32[]{:S(2)}) async-start(), calls=%async_computation.15 | async-start | bytes 4325376 | tf_op jit(solution)/shard_map/all_gather | solution.py:94
  135.7 311.3 %all-gather.18.cloned.1.call-start = ((), (), s32[]{:S(2)}) async-start(), calls=%async_computation.13 | async-start | bytes 4718592 | tf_op jit(solution)/shard_map/all_gather | solution.py:110
  136.2 62.8 %copy-start.56 = (f32[256,128]{0,1:T(8,128)}, f32[256,128]{0,1:T(8,128)S(1)}, u32[]{:S(2)}) copy-start(f32[256,128]{0,1:T(8,128)S(1)} %get-tuple-element.70) | copy-start | bytes 393220
  136.2 70.0 %copy-start.31 = (f32[256,128]{0,1:T(8,128)}, f32[256,128]{0,1:T(8,128)S(1)}, u32[]{:S(2)}) copy-start(f32[256,128]{0,1:T(8,128)S(1)} %get-tuple-element.69) | copy-start | bytes 393220
  137.4 380.4 %all-gather.26.cloned.1.call-start = ((), (), s32[]{:S(2)}) async-start(), calls=%async_computation.17 | async-start | bytes 6488064 | tf_op jit(solution)/shard_map/all_gather | solution.py:133
  138.1 450.5 %all-gather.24.cloned.1.call-start = ((), (), s32[]{:S(2)}) async-start(), calls=%async_computation.16 | async-start | bytes 6488064 | tf_op jit(solution)/shard_map/all_gather | solution.py:132
  138.7 520.9 %all-gather.28.cloned.1.call-start = ((), (), s32[]{:S(2)}) async-start(), calls=%async_computation.18 | async-start | bytes 6488064 | tf_op jit(solution)/shard_map/all_gather | solution.py:134
  139.4 809.5 %reduce-scatter.14.cloned.1.call-start = ((), (), s32[]{:S(2)}) async-start(), calls=%async_computation.21 | async-start | bytes 4718592 | tf_op jit(solution)/shard_map/reduce_scatter | solution.py:203
  139.7 65.0 %copy-start.99 = (f32[128]{0:T(128)}, f32[128]{0:T(128)S(1)}, u32[]{:S(2)}) copy-start(f32[128]{0:T(128)S(1)} %convert_element_type.367) | copy-start | bytes 1540
  207.3 239.8 %copy-start.18 = (bf16[256,16,128]{0,2,1:T(8,128)(2,1)}, bf16[256,16,128]{0,2,1:T(8,128)(2,1)S(1)}, u32[]{:S(2)}) copy-start(bf16[256,16,128]{0,2,1:T(8,128)(2,1)S(1)} %fusion.29) | copy-start | bytes 3145732
  499.0 203.5 %copy-start.11 = (f32[256,1024]{1,0:T(8,128)}, f32[256,1024]{1,0:T(8,128)S(1)}, u32[]{:S(2)}) copy-start(f32[256,1024]{1,0:T(8,128)S(1)} %get-tuple-element.104) | copy-start | bytes 3145732
  499.2 89.4 %copy-start.25 = (bf16[256,1024]{1,0:T(8,128)(2,1)}, bf16[256,1024]{1,0:T(8,128)(2,1)S(1)}, u32[]{:S(2)}) copy-start(bf16[256,1024]{1,0:T(8,128)(2,1)S(1)} %multiply_convert_fusion.7) | copy-start | bytes 1572868
  703.1 179.9 %copy-start.13 = (f32[256,1024]{1,0:T(8,128)}, f32[256,1024]{1,0:T(8,128)S(1)}, u32[]{:S(2)}) copy-start(f32[256,1024]{1,0:T(8,128)S(1)} %get-tuple-element.60) | copy-start | bytes 3145732
  709.2 16.8 copy-start.41
  726.0 226.8 %reduce-scatter.18.cloned.1.call-start = ((), (), s32[]{:S(2)}) async-start(), calls=%async_computation.23 | async-start | bytes 4718592 | tf_op jit(solution)/shard_map/reduce_scatter | solution.py:203
  748.6 209.7 %reduce-scatter.16.cloned.1.call-start = ((), (), s32[]{:S(2)}) async-start(), calls=%async_computation.22 | async-start | bytes 4718592 | tf_op jit(solution)/shard_map/reduce_scatter | solution.py:197
  774.5 28.9 %copy-start.20 = (bf16[256,16,128]{0,2,1:T(8,128)(2,1)S(1)}, bf16[256,16,128]{0,2,1:T(8,128)(2,1)}, u32[]{:S(2)}) copy-start(bf16[256,16,128]{0,2,1:T(8,128)(2,1)} %fusion.31) | copy-start | bytes 3145732
  813.9 146.8 %reduce-scatter.12.cloned.1.call-start = ((), (), s32[]{:S(2)}) async-start(), calls=%async_computation.20 | async-start | bytes 4718592 | tf_op jit(solution)/shard_map/reduce_scatter | solution.py:197
  840.7 29.0 %copy-start.19 = (bf16[256,16,128]{0,2,1:T(8,128)(2,1)S(1)}, bf16[256,16,128]{0,2,1:T(8,128)(2,1)}, u32[]{:S(2)}) copy-start(bf16[256,16,128]{0,2,1:T(8,128)(2,1)} %copy-done.18) | copy-start | bytes 3145732
  880.2 202.4 %reduce-scatter.26.cloned.1.call-start = ((), (), s32[]{:S(2)}) async-start(), calls=%async_computation.27 | async-start | bytes 8650752 | tf_op jit(solution)/shard_map/reduce_scatter | solution.py:263
  887.6 354.6 %reduce-scatter.30.cloned.1.call-start = ((), (), s32[]{:S(2)}) async-start(), calls=%async_computation.29 | async-start | bytes 12976128 | tf_op jit(solution)/shard_map/reduce_scatter | solution.py:262
  897.5 506.9 %reduce-scatter.28.cloned.1.call-start = ((), (), s32[]{:S(2)}) async-start(), calls=%async_computation.28 | async-start | bytes 12976128 | tf_op jit(solution)/shard_map/reduce_scatter | solution.py:262
  907.5 658.3 %reduce-scatter.32.cloned.1.call-start = ((), (), s32[]{:S(2)}) async-start(), calls=%async_computation.30 | async-start | bytes 12976128 | tf_op jit(solution)/shard_map/reduce_scatter | solution.py:262
  917.6 10.0 copy-start.55
  917.6 802.0 %reduce-scatter.20.cloned.1.call-start = ((), (), s32[]{:S(2)}) async-start(), calls=%async_computation.24 | async-start | bytes 8650752 | tf_op jit(solution)/shard_map/reduce_scatter | solution.py:263
  917.8 10.3 slice-start
  917.8 10.3 slice-start.1
  917.8 11.0 slice-start.2
  948.9 914.6 %reduce-scatter.24.cloned.1.call-start = ((), (), s32[]{:S(2)}) async-start(), calls=%async_computation.26 | async-start | bytes 4325376 | tf_op jit(solution)/shard_map/reduce_scatter | solution.py:263
  958.0 1047.7 %reduce-scatter.22.cloned.1.call-start = ((), (), s32[]{:S(2)}) async-start(), calls=%async_computation.25 | async-start | bytes 4325376 | tf_op jit(solution)/shard_map/reduce_scatter | solution.py:263
  988.4 45.1 %copy-start.96 = (f32[256]{0:T(256)S(1)}, f32[256]{0:T(256)}, u32[]{:S(2)}) copy-start(f32[256]{0:T(256)} %copy-done.95) | copy-start | bytes 3076
  988.4 45.1 %copy-start.98 = (f32[256]{0:T(256)S(1)}, f32[256]{0:T(256)}, u32[]{:S(2)}) copy-start(f32[256]{0:T(256)} %copy-done.97) | copy-start | bytes 3076
  988.4 45.1 %copy-start.14 = (f32[256,1024]{1,0:T(8,128)S(1)}, f32[256,1024]{1,0:T(8,128)}, u32[]{:S(2)}) copy-start(f32[256,1024]{1,0:T(8,128)} %copy-done.13) | copy-start | bytes 3145732
  988.4 45.2 %copy-start.17 = (f32[256,1024]{1,0:T(8,128)S(1)}, f32[256,1024]{1,0:T(8,128)}, u32[]{:S(2)}) copy-start(f32[256,1024]{1,0:T(8,128)} %copy-done.15) | copy-start | bytes 3145732
  (88 other events, 214.0 us)
Sparse Core Ops, SparseCore 0:
  11.0 59.1 all-gather.15
  73.2 55.3 all-gather.13
  131.6 60.9 all-gather.19
  194.0 46.3 all-gather.29
  242.5 45.3 all-gather.33
  289.3 45.8 all-gather.31
  338.2 60.8 all-gather.21
  400.7 46.3 all-gather.17
  450.1 67.6 all-gather.25
  520.6 67.9 all-gather.23
  591.6 67.9 all-gather.27
  726.1 48.4 reduce-scatter.13
  776.9 48.1 reduce-scatter.17
  827.3 48.1 reduce-scatter.15
  880.4 49.2 reduce-scatter.11
  932.4 150.2 reduce-scatter.25
  1089.1 153.0 reduce-scatter.29
  1249.7 154.7 reduce-scatter.27
  1411.0 154.7 reduce-scatter.31
  1568.7 150.9 reduce-scatter.19
  1722.6 140.8 reduce-scatter.23
  1866.4 139.3 reduce-scatter.21
where the time goes:
time: 2020 us; the launch traced here: 2010 us
  waiting for transfers between devices  1410 us (70%)
  matrix products  342 us (17%)
  other arithmetic  114 us (6%)
  blocking collectives  82.9 us (4%)
  local copies, waits for them, and re-layouts  47.1 us (2%)
    reduce_scatter x4, waiting for transfers between devices, shards(): lax.psum_scatter(attn_totals, ('dp', 'ctx'), scatter_dimension=0, tiled=T...  486 us
    reduce_scatter x3, waiting for transfers between devices, shards(): lax.psum_scatter(mlp_totals, ('dp', 'ctx'), scatter_dimension=0, tiled=True)  483 us
    unnamed x2, blocking collectives  82.9 us
    all_gather x2, waiting for transfers between devices, shards(): lax.all_gather(keys_own.reshape(SEQ_MB, shard_slots, KV * HD), 'ctx', axi...  74.9 us
    all_gather x1, waiting for transfers between devices, shards(): lax.all_gather(w_down, ('dp', 'ctx'), axis=0, tiled=True)  64.7 us
    all_gather x1, waiting for transfers between devices, shards(): lax.all_gather(w_gate, ('dp', 'ctx'), axis=0, tiled=True)  64.5 us
    all_gather x2, waiting for transfers between devices, shards(): lax.all_gather(values_own.reshape(SEQ_MB, shard_slots, KV * HD), 'ctx', a...  59 us
    another operation x2, other arithmetic  57.9 us
  transfers between devices with their start and end apart: 22, of which 18 were waited for; matrix products, arithmetic and copies ran while one was open for 21% of the time, Pallas kernels for 0%

commit v1 on v0

--- a/solution.py
+++ b/solution.py
@@ -12,6 +12,27 @@
 EPSILON = 1e-06
 THETA = 1000000.0
 NEGATIVE = -1e30
+
+
+def collect(value, axis, dim):
+    size, position, rows = (lax.axis_size(axis), lax.axis_index(axis), value.shape[dim])
+    right = [(i, (i + 1) % size) for i in range(size)]
+    left = [(i, (i - 1) % size) for i in range(size)]
+    whole = jnp.zeros((*value.shape[:dim], size * rows, *value.shape[dim + 1 :]), value.dtype)
+    whole = lax.dynamic_update_slice_in_dim(whole, value, position * rows, axis=dim)
+    from_left = from_right = value
+    half = size // 2
+    for lap in range(1, half + 1):
+        from_left = lax.ppermute(from_left, axis, right)
+        whole = lax.dynamic_update_slice_in_dim(
+            whole, from_left, (position - lap) % size * rows, axis=dim
+        )
+        if lap < size - half:
+            from_right = lax.ppermute(from_right, axis, left)
+            whole = lax.dynamic_update_slice_in_dim(
+                whole, from_right, (position + lap) % size * rows, axis=dim
+            )
+    return whole
 
 
 def normed(values, weights):
@@ -110,9 +131,7 @@
             lax.all_gather(
                 keys_own.reshape(SEQ_MB, shard_slots, KV * HD), "ctx", axis=1, tiled=True
             ),
-            lax.all_gather(
-                values_own.reshape(SEQ_MB, shard_slots, KV * HD), "ctx", axis=1, tiled=True
-            ),
+            collect(values_own.reshape(SEQ_MB, shard_slots, KV * HD), "ctx", 1),
         )
         keys_all = keys_all.reshape(SEQ_MB, SEQ, KV, HD)
         values_all = values_all.reshape(SEQ_MB, SEQ, KV, HD)

time: 2020 us -> 1960 us (0.970)
  waiting for transfers between devices: 1410 us -> 1290 us
  local copies, waits for them, and re-layouts: 47.1 us -> 80.9 us
    ppermute x0 -> x14, waiting for transfers between devices: none -> 63.1 us  [the longest x8 35.6 us: collect(): from_left = lax.ppermute(from_left, axis, right)]
    all_gather x2 -> x0, waiting for transfers between devices: 59 us -> none  [shards(): lax.all_gather(values_own.reshape(SEQ_MB, shard_slots, KV * HD), 'ctx', a...]
    all_gather x1, waiting for transfers between devices: 52 us -> 0.01 us  [shards(): lax.all_gather(w_query, ('dp', 'ctx'), axis=0, tiled=True)]
    all_gather x1, waiting for transfers between devices: 41 us -> 7.65 us  [shards(): lax.all_gather(w_out, ('dp', 'ctx'), axis=0, tiled=True)]
    all_gather x2, waiting for transfers between devices: 74.9 us -> 42.9 us  [shards(): lax.all_gather(keys_own.reshape(SEQ_MB, shard_slots, KV * HD), 'ctx', axi...]
  transfers between devices with their start and end apart: 22 -> 34, of which waited for: 18 -> 22; matrix products, arithmetic and copies ran while one was open for 21% -> 23% of each run, Pallas kernels for 0% -> 0%
where the time goes in v1:
time: 1960 us; the launch traced here: 1940 us
  waiting for transfers between devices  1290 us (66%)
  matrix products  339 us (17%)
  other arithmetic  114 us (6%)
  blocking collectives  82.5 us (4%)
  local copies, waits for them, and re-layouts  80.9 us (4%)
  starting transfers between devices  20.4 us (1%)
    reduce_scatter x4, waiting for transfers between devices, shards(): lax.psum_scatter(attn_totals, ('dp', 'ctx'), scatter_dimension=0, tiled=T...  486 us
    reduce_scatter x3, waiting for transfers between devices, shards(): lax.psum_scatter(mlp_totals, ('dp', 'ctx'), scatter_dimension=0, tiled=True)  483 us
    unnamed x2, blocking collectives  82.5 us
    all_gather x1, waiting for transfers between devices, shards(): lax.all_gather(w_down, ('dp', 'ctx'), axis=0, tiled=True)  64.7 us
    all_gather x1, waiting for transfers between devices, shards(): lax.all_gather(w_gate, ('dp', 'ctx'), axis=0, tiled=True)  64.7 us
    another operation x2, other arithmetic  58.2 us
    dot_general x2, matrix products, shards(): jnp.einsum('bqkgd,bskd->bkgqs', grad_heads, values_all, preferred_element...  50.3 us
    all_gather x1, waiting for transfers between devices, shards(): lax.all_gather(w_value, ('dp', 'ctx'), axis=0, tiled=True)  44.7 us
  transfers between devices with their start and end apart: 34, of which 22 were waited for; matrix products, arithmetic and copies ran while one was open for 23% of the time, Pallas kernels for 0%

profile of v1, /device:TPU:0, one launch (start us, length us, event | category | flops | bytes accessed | tf_op | source)
XLA Modules:
  0.0 1944.9 jit_solution(1017738728960833070)
XLA Ops:
  12.9 42.3 %all-reduce.17 = (bf16[1024]{0:T(1024)(128)(2,1)S(1)}, bf16[128]{0:T(256)(128)(2,1)S(1)}, bf16[128]{0:T(256)(128)(2,1)}, bf16[1024]{0:T(1024)(128)(2,1)}) all-reduce(bf16[1024]{0:T(1024)(128)(2,1)S(1)} %dynamic-update-slice, bf16[128]{0:T(256)(128)(2,1)S(1)} %dynamic-update-slice.1, ...), channel_id=1, replica_groups=mesh['dp'=4,'ctx'=8] {'dp','ctx'}, use_global_device_ids=true, to_apply=%add.8 | all-reduce | flops 2304 | bytes 9216
  59.3 10.9 all-gather.12.cloned.1.call-done
  83.9 44.7 %all-gather.10.cloned.1.call-done = bf16[1024,1024]{1,0:T(8,128)(2,1)} async-done(((bf16[32,1024]{1,0:T(8,128)(2,1)}), bf16[1024,1024]{1,0:T(8,128)(2,1)}) %all-gather.10.cloned.1.call-update) | async-done | bytes 2097168 | tf_op jit(solution)/shard_map/all_gather | solution.py:114
  143.6 12.7 collective-permute-done
  164.5 6.2 collective-permute-done.8
  193.9 8.7 collective-permute-done.10
  224.4 12.6 collective-permute-done.12
  244.9 14.1 collective-permute-done.6
  261.1 6.6 copy.92
  277.1 15.5 fusion.9
  292.6 14.5 exponential_reduce_fusion
  307.1 17.5 convolution_convert_fusion.2
  324.6 7.7 all-gather.18.cloned.1.call-done
  337.1 42.9 %all-gather.14.cloned.1.call-done = bf16[1,2048,1024]{1,2,0:T(8,128)(2,1)} async-done(((bf16[1,256,1024]{1,2,0:T(8,128)(2,1)}), bf16[1,2048,1024]{1,2,0:T(8,128)(2,1)}) %all-gather.14.cloned.1.call-update) | async-done | bytes 4194320 | tf_op jit(solution)/shard_map/all_gather | solution.py:131
  380.0 16.3 fusion.8
  396.3 14.5 exponential_reduce_fusion.1
  410.8 16.7 convolution_convert_fusion.3
  431.6 19.1 all-gather.22.cloned.1.call-done
  450.7 6.3 fusion.165
  457.0 64.7 %all-gather.20.cloned.1.call-done = bf16[1024,3072]{1,0:T(8,128)(2,1)} async-done(((bf16[32,3072]{1,0:T(8,128)(2,1)}), bf16[1024,3072]{1,0:T(8,128)(2,1)}) %all-gather.20.cloned.1.call-update) | async-done | bytes 6291472 | tf_op jit(solution)/shard_map/all_gather | solution.py:151
  521.7 6.3 fusion.164
  527.9 64.7 %all-gather.24.cloned.1.call-done = bf16[3072,1024]{1,0:T(8,128)(2,1)} async-done(((bf16[96,1024]{1,0:T(8,128)(2,1)}), bf16[3072,1024]{1,0:T(8,128)(2,1)}) %all-gather.24.cloned.1.call-update) | async-done | bytes 6291472 | tf_op jit(solution)/shard_map/all_gather | solution.py:153
  592.7 9.0 multiply_convert_fusion.2
  603.7 6.4 multiply_reduce_fusion.9
  617.6 9.6 multiply_convert_fusion
  627.2 5.7 fusion.170
  642.4 16.8 bitcast_convert_fusion.1
  665.2 16.6 bitcast_convert_fusion
  681.9 25.2 %fusion = (f32[8,2,256]{2,1,0:T(2,128)S(1)}, f32[8,2048,256,2]{2,1,3,0:T(8,128)}) fusion(f32[8,2048,256,2]{2,1,3,0:T(8,128)} %get-tuple-element.100, f32[8,2,256]{2,1,0:T(2,128)S(1)} %bitcast.480, pred[256,2048]{0,1:T(8,128)(4,1)S(1)} %broadcast_compare_fusion, bf16[2048,8,128,1]{0,2,3,1:T(8,128)(2,1)} %bitcast.28, bf16[256,8,2,128]{0,3,2,1:T(8,128)(2,1)S(1)} %bitcast.454), kind=kOutput, calls=%fused_computation.4 | convolution fusion | flops 2189422592 | bytes 72908800 | tf_op jit(solution)/shard_map/bqkgd,bskd->bkgqs/dot_general | solution.py:200
  707.1 29.1 %fusion.13 = bf16[8,2,256,2048]{2,3,1,0:T(8,128)(2,1)} fusion(f32[8,2048,256,2]{2,1,3,0:T(8,128)} %get-tuple-element.112, f32[8,2048,256,2]{2,1,3,0:T(8,128)} %get-tuple-element.100, f32[8,2,256]{2,1,0:T(2,128)S(1)} %get-tuple-element.111, f32[8,2,256]{2,1,0:T(2,128)S(1)} %bitcast.481, pred[256,2048]{0,1:T(8,128)(4,1)S(1)} %broadcast_compare_fusion), kind=kLoop, calls=%fused_computation.23 | loop fusion | flops 50331648 | bytes 84443136 | tf_op jit(solution)/shard_map/reshape.45
  736.3 10.5 fusion.14
  748.0 25.1 %fusion.3 = (f32[8,2,256]{2,1,0:T(2,128)S(1)}, f32[8,2048,256,2]{2,1,3,0:T(8,128)}) fusion(f32[8,2048,256,2]{2,1,3,0:T(8,128)} %get-tuple-element.102, f32[8,2,256]{2,1,0:T(2,128)S(1)} %bitcast.476, pred[256,2048]{0,1:T(8,128)(4,1)S(1)} %broadcast_compare_fusion.1, bf16[2048,8,128,1]{0,2,3,1:T(8,128)(2,1)} %bitcast.4, bf16[256,8,2,128]{0,3,2,1:T(8,128)(2,1)S(1)} %bitcast.452), kind=kOutput, calls=%fused_computation.9 | convolution fusion | flops 2189422592 | bytes 72908800 | tf_op jit(solution)/shard_map/bqkgd,bskd->bkgqs/dot_general | solution.py:200
  773.1 29.1 %fusion.12 = bf16[8,2,256,2048]{2,3,1,0:T(8,128)(2,1)} fusion(f32[8,2048,256,2]{2,1,3,0:T(8,128)} %get-tuple-element.110, f32[8,2048,256,2]{2,1,3,0:T(8,128)} %get-tuple-element.102, f32[8,2,256]{2,1,0:T(2,128)S(1)} %get-tuple-element.109, f32[8,2,256]{2,1,0:T(2,128)S(1)} %bitcast.477, pred[256,2048]{0,1:T(8,128)(4,1)S(1)} %broadcast_compare_fusion.1), kind=kLoop, calls=%fused_computation.22 | loop fusion | flops 50331648 | bytes 84443136 | tf_op jit(solution)/shard_map/reshape.28
  802.2 10.5 fusion.15
  823.4 6.5 convolution_add_fusion.1
  833.4 6.5 convolution_add_fusion.2
  843.6 6.5 convolution_add_fusion
  850.3 9.7 convolution_multiply_fusion
  885.3 5.2 convolution_add_fusion.5
  903.1 5.3 fusion.45
  923.1 40.2 %all-reduce.16 = (f32[1024]{0:T(1024)S(1)}, f32[1024]{0:T(1024)S(1)}, f32[128]{0:T(128)S(1)}, f32[128]{0:T(128)S(1)}) all-reduce(f32[1024]{0:T(1024)S(1)} %add.385, f32[1024]{0:T(1024)S(1)} %add.386, f32[128]{0:T(128)S(1)} %add.387, f32[128]{0:T(128)S(1)} %add.388), channel_id=13, replica_groups=mesh['dp'=4,'ctx'=8] {'dp','ctx'}, use_global_device_ids=true, to_apply=%region_35.36.clone | all-reduce | flops 2304 | bytes 18432
  968.9 46.2 %reduce-scatter.26.cloned.1.call-done = f32[64,1024]{1,0:T(8,128)} async-done(((f32[2048,1024]{1,0:T(8,128)}), f32[64,1024]{1,0:T(8,128)}) %reduce-scatter.26.cloned.1.call-update) | async-done | bytes 262160 | tf_op jit(solution)/shard_map/reduce_scatter | solution.py:282
  1015.1 159.7 %reduce-scatter.30.cloned.1.call-done = f32[32,3072]{1,0:T(8,128)} async-done(((f32[1024,3072]{1,0:T(8,128)}), f32[32,3072]{1,0:T(8,128)}) %reduce-scatter.30.cloned.1.call-update) | async-done | bytes 393232 | tf_op jit(solution)/shard_map/reduce_scatter | solution.py:281
  1174.8 162.0 %reduce-scatter.28.cloned.1.call-done = f32[32,3072]{1,0:T(8,128)} async-done(((f32[1024,3072]{1,0:T(8,128)}), f32[32,3072]{1,0:T(8,128)}) %reduce-scatter.28.cloned.1.call-update) | async-done | bytes 393232 | tf_op jit(solution)/shard_map/reduce_scatter | solution.py:281
  1336.8 161.0 %reduce-scatter.32.cloned.1.call-done = f32[96,1024]{1,0:T(8,128)} async-done(((f32[3072,1024]{1,0:T(8,128)}), f32[96,1024]{1,0:T(8,128)}) %reduce-scatter.32.cloned.1.call-update) | async-done | bytes 393232 | tf_op jit(solution)/shard_map/reduce_scatter | solution.py:281
  1497.8 154.8 %reduce-scatter.20.cloned.1.call-done = f32[32,2048]{1,0:T(8,128)} async-done(((f32[1024,2048]{1,0:T(8,128)}), f32[32,2048]{1,0:T(8,128)}) %reduce-scatter.20.cloned.1.call-update) | async-done | bytes 262160 | tf_op jit(solution)/shard_map/reduce_scatter | solution.py:282
  1652.6 142.8 %reduce-scatter.24.cloned.1.call-done = f32[32,1024]{1,0:T(8,128)} async-done(((f32[1024,1024]{1,0:T(8,128)}), f32[32,1024]{1,0:T(8,128)}) %reduce-scatter.24.cloned.1.call-update) | async-done | bytes 131088 | tf_op jit(solution)/shard_map/reduce_scatter | solution.py:282
  1795.4 142.3 %reduce-scatter.22.cloned.1.call-done = f32[32,1024]{1,0:T(8,128)} async-done(((f32[1024,1024]{1,0:T(8,128)}), f32[32,1024]{1,0:T(8,128)}) %reduce-scatter.22.cloned.1.call-update) | async-done | bytes 131088 | tf_op jit(solution)/shard_map/reduce_scatter | solution.py:282
  (462 shorter events, 220.4 us)
Async XLA Ops:
  7.2 67.1 %copy-start = (bf16[2,256,1024]{2,1,0:T(8,128)(2,1)S(1)}, bf16[2,256,1024]{2,1,0:T(8,128)(2,1)}, u32[]{:S(2)}) copy-start(bf16[2,256,1024]{2,1,0:T(8,128)(2,1)} %param.14) | copy-start | bytes 3145732
  7.2 63.1 %all-gather.12.cloned.1.call-start = ((), (), s32[]{:S(2)}) async-start(), calls=%async_computation.12 | async-start | bytes 2162688 | tf_op jit(solution)/shard_map/all_gather | solution.py:113
  7.9 120.7 %all-gather.10.cloned.1.call-start = ((), (), s32[]{:S(2)}) async-start(), calls=%async_computation.11 | async-start | bytes 2162688 | tf_op jit(solution)/shard_map/all_gather | solution.py:114
  8.7 252.4 %all-gather.16.cloned.1.call-start = ((), (), s32[]{:S(2)}) async-start(), calls=%async_computation.14 | async-start | bytes 4325376 | tf_op jit(solution)/shard_map/all_gather | solution.py:112
  9.4 267.7 %all-gather.26.cloned.1.call-start = ((), (), s32[]{:S(2)}) async-start(), calls=%async_computation.19 | async-start | bytes 4718592 | tf_op jit(solution)/shard_map/all_gather | solution.py:131
  55.1 216.4 %copy-start.71 = (f32[1024]{0:T(1024)}, f32[1024]{0:T(1024)S(1)}, u32[]{:S(2)}) copy-start(f32[1024]{0:T(1024)S(1)} %convert_element_type.356) | copy-start | bytes 12292
  57.2 218.5 %copy-start.29 = (f32[256,128]{0,1:T(8,128)}, f32[256,128]{0,1:T(8,128)S(1)}, u32[]{:S(2)}) copy-start(f32[256,128]{0,1:T(8,128)S(1)} %get-tuple-element.71) | copy-start | bytes 393220
  57.2 218.5 %copy-start.54 = (f32[256,128]{0,1:T(8,128)}, f32[256,128]{0,1:T(8,128)S(1)}, u32[]{:S(2)}) copy-start(f32[256,128]{0,1:T(8,128)S(1)} %get-tuple-element.72) | copy-start | bytes 393220
  59.3 212.2 %copy-start.87 = (f32[256]{0:T(256)}, f32[256]{0:T(256)S(1)}, u32[]{:S(2)}) copy-start(f32[256]{0:T(256)S(1)} %fusion.135) | copy-start | bytes 3076
  79.3 253.0 %all-gather.18.cloned.1.call-start = ((), (), s32[]{:S(2)}) async-start(), calls=%async_computation.15 | async-start | bytes 4325376 | tf_op jit(solution)/shard_map/all_gather | solution.py:115
  79.9 300.2 %all-gather.14.cloned.1.call-start = ((), (), s32[]{:S(2)}) async-start(), calls=%async_computation.13 | async-start | bytes 4718592 | tf_op jit(solution)/shard_map/all_gather | solution.py:131
  80.4 194.3 %copy-start.31 = (f32[256,128]{0,1:T(8,128)}, f32[256,128]{0,1:T(8,128)S(1)}, u32[]{:S(2)}) copy-start(f32[256,128]{0,1:T(8,128)S(1)} %get-tuple-element.69) | copy-start | bytes 393220
  81.5 53.3 %copy-start.86 = (s32[1,2048]{1,0:T(1,128)S(1)}, s32[1,2048]{1,0:T(1,128)}, u32[]{:S(2)}) copy-start(s32[1,2048]{1,0:T(1,128)} %copy-done.85) | copy-start | bytes 24580
  81.5 369.2 %all-gather.22.cloned.1.call-start = ((), (), s32[]{:S(2)}) async-start(), calls=%async_computation.17 | async-start | bytes 6488064 | tf_op jit(solution)/shard_map/all_gather | solution.py:152
  82.3 439.4 %all-gather.20.cloned.1.call-start = ((), (), s32[]{:S(2)}) async-start(), calls=%async_computation.16 | async-start | bytes 6488064 | tf_op jit(solution)/shard_map/all_gather | solution.py:151
  83.0 509.6 %all-gather.24.cloned.1.call-start = ((), (), s32[]{:S(2)}) async-start(), calls=%async_computation.18 | async-start | bytes 6488064 | tf_op jit(solution)/shard_map/all_gather | solution.py:153
  83.8 58.5 %copy-start.99 = (s32[1,256]{1,0:T(1,128)S(1)}, s32[1,256]{1,0:T(1,128)}, u32[]{:S(2)}) copy-start(s32[1,256]{1,0:T(1,128)} %copy-done.98) | copy-start | bytes 3076
  83.8 59.1 %copy-start.116 = (bf16[128]{0:T(256)(128)(2,1)S(1)}, bf16[128]{0:T(256)(128)(2,1)}, u32[]{:S(2)}) copy-start(bf16[128]{0:T(256)(128)(2,1)} %get-tuple-element.39) | copy-start | bytes 772
  83.8 59.6 %copy-start.111 = (bf16[1024]{0:T(1024)(128)(2,1)S(1)}, bf16[1024]{0:T(1024)(128)(2,1)}, u32[]{:S(2)}) copy-start(bf16[1024]{0:T(1024)(128)(2,1)} %get-tuple-element.40) | copy-start | bytes 6148
  83.8 797.6 %reduce-scatter.14.cloned.1.call-start = ((), (), s32[]{:S(2)}) async-start(), calls=%async_computation.21 | async-start | bytes 4718592 | tf_op jit(solution)/shard_map/reduce_scatter | solution.py:222
  131.0 11.3 collective-permute-start.7
  134.4 21.9 %collective-permute-start = (bf16[1,256,1024]{2,1,0:T(8,128)(2,1)}, bf16[1,256,1024]{2,1,0:T(8,128)(2,1)}, u32[]{:S(2)}, u32[]{:S(2)}) collective-permute-start(bf16[1,256,1024]{2,1,0:T(8,128)(2,1)} %fusion.46), channel_id=1, source_target_pairs={{0,1},{1,2},{2,3},{3,4},{4,5},{5,6},{6,7},{7,0},{8,9},{9,10},{10,1... | collective-permute-start | bytes 1572872 | tf_op jit(solution)/shard_map/ppermute | solution.py:26
  135.3 25.6 %collective-permute-start.1 = (bf16[1,256,1024]{2,1,0:T(8,128)(2,1)}, bf16[1,256,1024]{2,1,0:T(8,128)(2,1)}, u32[]{:S(2)}, u32[]{:S(2)}) collective-permute-start(bf16[1,256,1024]{2,1,0:T(8,128)(2,1)} %fusion.46), channel_id=1, source_target_pairs={{0,7},{1,0},{2,1},{3,2},{4,3},{5,4},{6,5},{7,6},{8,15},{9,8},{10,9... | collective-permute-start | bytes 1572872 | tf_op jit(solution)/shard_map/ppermute | solution.py:31
  138.5 32.1 %collective-permute-start.8 = (bf16[1,256,1024]{2,1,0:T(8,128)(2,1)S(1)}, bf16[1,256,1024]{2,1,0:T(8,128)(2,1)}, u32[]{:S(2)}, u32[]{:S(2)}) collective-permute-start(bf16[1,256,1024]{2,1,0:T(8,128)(2,1)S(1)} %fusion.47), channel_id=1, source_target_pairs={{0,7},{1,0},{2,1},{3,2},{4,3},{5,4},{6,5},{7,6},{8,15},{9,8},{10,9... | collective-permute-start | bytes 1572872 | tf_op jit(solution)/shard_map/ppermute | solution.py:31
  142.3 42.8 %collective-permute-start.9 = (bf16[1,256,1024]{2,1,0:T(8,128)(2,1)}, bf16[1,256,1024]{2,1,0:T(8,128)(2,1)}, u32[]{:S(2)}, u32[]{:S(2)}) collective-permute-start(bf16[1,256,1024]{2,1,0:T(8,128)(2,1)} %collective-permute-done.7), channel_id=1, source_target_pairs={{0,1},{1,2},{2,3},{3,4},{4,5},{5,6},{6,7},{7,0},{8,9},{9,10},{10,1... | collective-permute-start | bytes 1572872 | tf_op jit(solution)/shard_map/ppermute | solution.py:26
  156.3 31.9 %collective-permute-start.2 = (bf16[1,256,1024]{2,1,0:T(8,128)(2,1)}, bf16[1,256,1024]{2,1,0:T(8,128)(2,1)}, u32[]{:S(2)}, u32[]{:S(2)}) collective-permute-start(bf16[1,256,1024]{2,1,0:T(8,128)(2,1)} %collective-permute-done), channel_id=1, source_target_pairs={{0,1},{1,2},{2,3},{3,4},{4,5},{5,6},{6,7},{7,0},{8,9},{9,10},{10,1... | collective-permute-start | bytes 1572872 | tf_op jit(solution)/shard_map/ppermute | solution.py:26
  160.9 29.4 %collective-permute-start.3 = (bf16[1,256,1024]{2,1,0:T(8,128)(2,1)}, bf16[1,256,1024]{2,1,0:T(8,128)(2,1)}, u32[]{:S(2)}, u32[]{:S(2)}) collective-permute-start(bf16[1,256,1024]{2,1,0:T(8,128)(2,1)} %collective-permute-done.1), channel_id=1, source_target_pairs={{0,7},{1,0},{2,1},{3,2},{4,3},{5,4},{6,5},{7,6},{8,15},{9,8},{10,9... | collective-permute-start | bytes 1572872 | tf_op jit(solution)/shard_map/ppermute | solution.py:31
  170.6 31.9 %collective-permute-start.10 = (bf16[1,256,1024]{2,1,0:T(8,128)(2,1)}, bf16[1,256,1024]{2,1,0:T(8,128)(2,1)}, u32[]{:S(2)}, u32[]{:S(2)}) collective-permute-start(bf16[1,256,1024]{2,1,0:T(8,128)(2,1)} %collective-permute-done.8), channel_id=1, source_target_pairs={{0,7},{1,0},{2,1},{3,2},{4,3},{5,4},{6,5},{7,6},{8,15},{9,8},{10,9... | collective-permute-start | bytes 1572872 | tf_op jit(solution)/shard_map/ppermute | solution.py:31
  185.1 29.4 %collective-permute-start.11 = (bf16[1,256,1024]{2,1,0:T(8,128)(2,1)}, bf16[1,256,1024]{2,1,0:T(8,128)(2,1)}, u32[]{:S(2)}, u32[]{:S(2)}) collective-permute-start(bf16[1,256,1024]{2,1,0:T(8,128)(2,1)} %collective-permute-done.9), channel_id=1, source_target_pairs={{0,1},{1,2},{2,3},{3,4},{4,5},{5,6},{6,7},{7,0},{8,9},{9,10},{10,1... | collective-permute-start | bytes 1572872 | tf_op jit(solution)/shard_map/ppermute | solution.py:26
  188.2 32.9 %collective-permute-start.4 = (bf16[1,256,1024]{2,1,0:T(8,128)(2,1)}, bf16[1,256,1024]{2,1,0:T(8,128)(2,1)}, u32[]{:S(2)}, u32[]{:S(2)}) collective-permute-start(bf16[1,256,1024]{2,1,0:T(8,128)(2,1)} %collective-permute-done.2), channel_id=1, source_target_pairs={{0,1},{1,2},{2,3},{3,4},{4,5},{5,6},{6,7},{7,0},{8,9},{9,10},{10,1... | collective-permute-start | bytes 1572872 | tf_op jit(solution)/shard_map/ppermute | solution.py:26
  190.3 32.8 %collective-permute-start.5 = (bf16[1,256,1024]{2,1,0:T(8,128)(2,1)}, bf16[1,256,1024]{2,1,0:T(8,128)(2,1)}, u32[]{:S(2)}, u32[]{:S(2)}) collective-permute-start(bf16[1,256,1024]{2,1,0:T(8,128)(2,1)} %collective-permute-done.3), channel_id=1, source_target_pairs={{0,7},{1,0},{2,1},{3,2},{4,3},{5,4},{6,5},{7,6},{8,15},{9,8},{10,9... | collective-permute-start | bytes 1572872 | tf_op jit(solution)/shard_map/ppermute | solution.py:31
  202.6 34.5 %collective-permute-start.12 = (bf16[1,256,1024]{2,1,0:T(8,128)(2,1)}, bf16[1,256,1024]{2,1,0:T(8,128)(2,1)}, u32[]{:S(2)}, u32[]{:S(2)}) collective-permute-start(bf16[1,256,1024]{2,1,0:T(8,128)(2,1)} %collective-permute-done.10), channel_id=1, source_target_pairs={{0,7},{1,0},{2,1},{3,2},{4,3},{5,4},{6,5},{7,6},{8,15},{9,8},{10,9... | collective-permute-start | bytes 1572872 | tf_op jit(solution)/shard_map/ppermute | solution.py:31
  214.5 28.2 %collective-permute-start.13 = (bf16[1,256,1024]{2,1,0:T(8,128)(2,1)}, bf16[1,256,1024]{2,1,0:T(8,128)(2,1)}, u32[]{:S(2)}, u32[]{:S(2)}) collective-permute-start(bf16[1,256,1024]{2,1,0:T(8,128)(2,1)} %collective-permute-done.11), channel_id=1, source_target_pairs={{0,1},{1,2},{2,3},{3,4},{4,5},{5,6},{6,7},{7,0},{8,9},{9,10},{10,1... | collective-permute-start | bytes 1572872 | tf_op jit(solution)/shard_map/ppermute | solution.py:26
  221.0 37.9 %collective-permute-start.6 = (bf16[1,256,1024]{2,1,0:T(8,128)(2,1)}, bf16[1,256,1024]{2,1,0:T(8,128)(2,1)}, u32[]{:S(2)}, u32[]{:S(2)}) collective-permute-start(bf16[1,256,1024]{2,1,0:T(8,128)(2,1)} %collective-permute-done.4), channel_id=1, source_target_pairs={{0,1},{1,2},{2,3},{3,4},{4,5},{5,6},{6,7},{7,0},{8,9},{9,10},{10,1... | collective-permute-start | bytes 1572872 | tf_op jit(solution)/shard_map/ppermute | solution.py:26
  275.7 104.3 %copy-start.18 = (bf16[256,16,128]{0,2,1:T(8,128)(2,1)}, bf16[256,16,128]{0,2,1:T(8,128)(2,1)S(1)}, u32[]{:S(2)}) copy-start(bf16[256,16,128]{0,2,1:T(8,128)(2,1)S(1)} %fusion.21) | copy-start | bytes 3145732
  431.4 204.2 %copy-start.11 = (f32[256,1024]{1,0:T(8,128)}, f32[256,1024]{1,0:T(8,128)S(1)}, u32[]{:S(2)}) copy-start(f32[256,1024]{1,0:T(8,128)S(1)} %get-tuple-element.104) | copy-start | bytes 3145732
  431.6 90.1 %copy-start.25 = (bf16[256,1024]{1,0:T(8,128)(2,1)}, bf16[256,1024]{1,0:T(8,128)(2,1)S(1)}, u32[]{:S(2)}) copy-start(bf16[256,1024]{1,0:T(8,128)(2,1)S(1)} %multiply_convert_fusion.7) | copy-start | bytes 1572868
  636.3 179.3 %copy-start.13 = (f32[256,1024]{1,0:T(8,128)}, f32[256,1024]{1,0:T(8,128)S(1)}, u32[]{:S(2)}) copy-start(f32[256,1024]{1,0:T(8,128)S(1)} %get-tuple-element.60) | copy-start | bytes 3145732
  659.2 226.1 %reduce-scatter.18.cloned.1.call-start = ((), (), s32[]{:S(2)}) async-start(), calls=%async_computation.23 | async-start | bytes 4718592 | tf_op jit(solution)/shard_map/reduce_scatter | solution.py:222
  681.9 209.0 %reduce-scatter.16.cloned.1.call-start = ((), (), s32[]{:S(2)}) async-start(), calls=%async_computation.22 | async-start | bytes 4718592 | tf_op jit(solution)/shard_map/reduce_scatter | solution.py:216
  746.8 146.4 %reduce-scatter.12.cloned.1.call-start = ((), (), s32[]{:S(2)}) async-start(), calls=%async_computation.20 | async-start | bytes 4718592 | tf_op jit(solution)/shard_map/reduce_scatter | solution.py:216
  812.8 202.4 %reduce-scatter.26.cloned.1.call-start = ((), (), s32[]{:S(2)}) async-start(), calls=%async_computation.27 | async-start | bytes 8650752 | tf_op jit(solution)/shard_map/reduce_scatter | solution.py:282
  820.1 354.8 %reduce-scatter.30.cloned.1.call-start = ((), (), s32[]{:S(2)}) async-start(), calls=%async_computation.29 | async-start | bytes 12976128 | tf_op jit(solution)/shard_map/reduce_scatter | solution.py:281
  830.0 506.8 %reduce-scatter.28.cloned.1.call-start = ((), (), s32[]{:S(2)}) async-start(), calls=%async_computation.28 | async-start | bytes 12976128 | tf_op jit(solution)/shard_map/reduce_scatter | solution.py:281
  840.0 657.8 %reduce-scatter.32.cloned.1.call-start = ((), (), s32[]{:S(2)}) async-start(), calls=%async_computation.30 | async-start | bytes 12976128 | tf_op jit(solution)/shard_map/reduce_scatter | solution.py:281
  850.1 802.5 %reduce-scatter.20.cloned.1.call-start = ((), (), s32[]{:S(2)}) async-start(), calls=%async_computation.24 | async-start | bytes 8650752 | tf_op jit(solution)/shard_map/reduce_scatter | solution.py:282
  881.4 914.0 %reduce-scatter.24.cloned.1.call-start = ((), (), s32[]{:S(2)}) async-start(), calls=%async_computation.26 | async-start | bytes 4325376 | tf_op jit(solution)/shard_map/reduce_scatter | solution.py:282
  890.6 1047.1 %reduce-scatter.22.cloned.1.call-start = ((), (), s32[]{:S(2)}) async-start(), calls=%async_computation.25 | async-start | bytes 4325376 | tf_op jit(solution)/shard_map/reduce_scatter | solution.py:282
  (109 other events, 681.6 us)
Sparse Core Ops, SparseCore 0:
  11.0 59.2 all-gather.11
  73.2 55.3 all-gather.9
  131.6 68.6 all-gather.15
  202.4 67.3 all-gather.25
  272.6 59.6 all-gather.17
  333.7 46.2 all-gather.13
  383.0 67.6 all-gather.21
  453.7 67.9 all-gather.19
  524.7 67.9 all-gather.23
  659.3 48.4 reduce-scatter.13
  710.1 48.1 reduce-scatter.17
  760.4 48.1 reduce-scatter.15
  812.9 48.9 reduce-scatter.11
  864.5 150.5 reduce-scatter.25
  1021.6 153.2 reduce-scatter.29
  1182.3 154.4 reduce-scatter.27
  1343.3 154.4 reduce-scatter.31
  1500.6 151.9 reduce-scatter.19
  1655.5 139.8 reduce-scatter.23
  1798.2 139.4 reduce-scatter.21
